TPU v7x, 32 devices: a whole 2x2x4 slice. The times are simulated.
32 devices in a mesh: dp: 8 (over z, x), ctx: 4 (over y, core).
Axes of the slice: x: 2, y: 2, z: 4, core: 2. Of those that a mesh axis runs over, the one named last changes fastest.
Arguments:
- tokens: bfloat16 [16, 2048, 768], P('dp', 'ctx'), may hold values from -6 to 6
- segments: int32 [16, 2048], P('dp'), may hold values from 0 to 4, never falling along the last dimension, each value on 1 to 800 neighbouring positions
- cotangent: bfloat16 [16, 2048, 768], P('dp', 'ctx'), may hold values from -6 to 6
- query_weight: bfloat16 [768, 768], P(('dp', 'ctx')), may hold values from -0.21875 to 0.21875
- query_bias: bfloat16 [768], P(('dp', 'ctx')), may hold values from -3 to 3
- key_weight: bfloat16 [768, 768], P(('dp', 'ctx')), may hold values from -0.21875 to 0.21875
- value_weight: bfloat16 [768, 768], P(('dp', 'ctx')), may hold values from -0.21875 to 0.21875
- value_bias: bfloat16 [768], P(('dp', 'ctx')), may hold values from -0.59765625 to 0.59765625
- output_weight: bfloat16 [768, 768], P(('dp', 'ctx')), may hold values from -0.875 to 0.875
- output_bias: bfloat16 [768], P(('dp', 'ctx')), may hold values from -2 to 2
- first_gain: bfloat16 [768], P(('dp', 'ctx')), may hold values from 0.5 to 1.5
- first_shift: bfloat16 [768], P(('dp', 'ctx')), may hold values from -2 to 2
- inner_weight: bfloat16 [768, 3072], P(('dp', 'ctx')), may hold values from -0.21875 to 0.21875
- inner_bias: bfloat16 [3072], P(('dp', 'ctx')), may hold values from -3 to 3
- outer_weight: bfloat16 [3072, 768], P(('dp', 'ctx')), may hold values from -0.109375 to 0.109375
- outer_bias: bfloat16 [768], P(('dp', 'ctx')), may hold values from -2 to 2
- second_gain: bfloat16 [768], P(('dp', 'ctx')), may hold values from 0.5 to 1.5
- second_shift: bfloat16 [768], P(('dp', 'ctx')), may hold values from -2 to 2
Outputs:
- layer_output: bfloat16 [16, 2048, 768], P('dp', 'ctx')
- input_gradient: float32 [16, 2048, 768], P('dp', 'ctx')
- query_weight_gradient: float32 [768, 768], P(('dp', 'ctx'))
- query_bias_gradient: float32 [768], P(('dp', 'ctx'))
- key_weight_gradient: float32 [768, 768], P(('dp', 'ctx'))
- value_weight_gradient: float32 [768, 768], P(('dp', 'ctx'))
- value_bias_gradient: float32 [768], P(('dp', 'ctx'))
- output_weight_gradient: float32 [768, 768], P(('dp', 'ctx'))
- output_bias_gradient: float32 [768], P(('dp', 'ctx'))
- first_gain_gradient: float32 [768], P(('dp', 'ctx'))
- first_shift_gradient: float32 [768], P(('dp', 'ctx'))
- inner_weight_gradient: float32 [768, 3072], P(('dp', 'ctx'))
- inner_bias_gradient: float32 [3072], P(('dp', 'ctx'))
- outer_weight_gradient: float32 [3072, 768], P(('dp', 'ctx'))
- outer_bias_gradient: float32 [768], P(('dp', 'ctx'))
- second_gain_gradient: float32 [768], P(('dp', 'ctx'))
- second_shift_gradient: float32 [768], P(('dp', 'ctx'))
Inputs may be any that keep to these rules, and one draw needn't show every extreme that they name: `segments`: in each sequence the document numbers start at 0 and never fall; a document has 1 to 800 tokens, one of each sequence exactly 800, and there are at most 5 documents.
All inputs are finite; a program needn't handle non-finite values.
Results may differ from a plain program's by a relative error of at most 0.028.
Values may be sent and summed in bfloat16 or wider, within the bound.
No kernel may reach another device: no remote copies, remote signals or barrier semaphores. Data moves between devices by JAX's collectives and lax.ppermute only.
A program may use at most 384 MiB of HBM per device.

v0:
```python
import math
import jax
import jax.numpy as jnp
from jax import lax
from jax.sharding import PartitionSpec as P

HEADS = 12
HEAD = 64
epsilon = 1e-05


def layer_norm(values, gain, shift):
    average = jnp.mean(values, axis=-1, keepdims=True)
    centred = values - average
    spread = jnp.mean(centred * centred, axis=-1, keepdims=True)
    return centred * lax.rsqrt(spread + epsilon) * gain + shift


def gelu_exact(values):
    return jax.nn.gelu(values, approximate=False)


def fetch_weights(shards):
    return (
        lax.all_gather(shards[0], ("dp", "ctx"), axis=0, tiled=True),
        lax.all_gather(shards[1], ("dp", "ctx"), axis=0, tiled=True),
        lax.all_gather(shards[2], ("dp", "ctx"), axis=0, tiled=True),
        lax.all_gather(shards[3], ("dp", "ctx"), axis=0, tiled=True),
        lax.all_gather(shards[4], ("dp", "ctx"), axis=0, tiled=True),
        lax.all_gather(shards[5], ("dp", "ctx"), axis=0, tiled=True),
        lax.all_gather(shards[6], ("dp", "ctx"), axis=0, tiled=True),
        lax.all_gather(shards[7], ("dp", "ctx"), axis=0, tiled=True),
        lax.all_gather(shards[8], ("dp", "ctx"), axis=0, tiled=True),
        lax.all_gather(shards[9], ("dp", "ctx"), axis=0, tiled=True),
        lax.all_gather(shards[10], ("dp", "ctx"), axis=0, tiled=True),
        lax.all_gather(shards[11], ("dp", "ctx"), axis=0, tiled=True),
        lax.all_gather(shards[12], ("dp", "ctx"), axis=0, tiled=True),
        lax.all_gather(shards[13], ("dp", "ctx"), axis=0, tiled=True),
        lax.all_gather(shards[14], ("dp", "ctx"), axis=0, tiled=True),
    )


def masked_scores(query_heads, key_heads, allowed, scale):
    scores = (
        jnp.einsum("qhd,khd->hqk", query_heads, key_heads, preferred_element_type=jnp.float32)
        * scale
    )
    return jnp.where(allowed, scores, -1e30)


def matmul(left, right):
    return jnp.dot(left, right, preferred_element_type=jnp.float32)


def column_sums(values):
    return jnp.sum(values.astype(jnp.float32), axis=0)


def on_device(
    tokens,
    segments,
    cotangent,
    query_weight,
    query_bias,
    key_weight,
    value_weight,
    value_bias,
    output_weight,
    output_bias,
    first_gain,
    first_shift,
    inner_weight,
    inner_bias,
    outer_weight,
    outer_bias,
    second_gain,
    second_shift,
):
    shards = (
        query_weight,
        query_bias,
        key_weight,
        value_weight,
        value_bias,
        output_weight,
        output_bias,
        first_gain,
        first_shift,
        inner_weight,
        inner_bias,
        outer_weight,
        outer_bias,
        second_gain,
        second_shift,
    )
    micro = tokens.shape[0]
    local = tokens.shape[1]
    width = tokens.shape[2]
    scale = 1.0 / math.sqrt(HEAD)
    offset = lax.axis_index("ctx") * local
    outputs = []
    input_grads = []
    totals = None
    for micro_step in range(micro):
        params = fetch_weights(shards)
        source = tokens[micro_step]
        seg_whole = segments[micro_step]
        seg_local = lax.dynamic_slice_in_dim(seg_whole, offset, local)
        allowed = seg_local[None, :, None] == seg_whole[None, None, :]
        queries = (matmul(source, params[0]) + params[1].astype(jnp.float32)).astype(jnp.bfloat16)
        keys_local = matmul(source, params[2]).astype(jnp.bfloat16)
        values_local = (matmul(source, params[3]) + params[4].astype(jnp.float32)).astype(
            jnp.bfloat16
        )
        keys_whole, values_whole = (
            lax.all_gather(keys_local, "ctx", axis=0, tiled=True),
            lax.all_gather(values_local, "ctx", axis=0, tiled=True),
        )
        query_heads = queries.reshape(local, HEADS, HEAD)
        key_heads = keys_whole.reshape(-1, HEADS, HEAD)
        value_heads = values_whole.reshape(-1, HEADS, HEAD)
        masked = masked_scores(query_heads, key_heads, allowed, scale)
        largest = jnp.max(masked, axis=-1, keepdims=True)
        logsum = largest + jnp.log(jnp.sum(jnp.exp(masked - largest), axis=-1, keepdims=True))
        probs_low = jnp.exp(masked - logsum).astype(jnp.bfloat16)
        mixed = (
            jnp.einsum("hqk,khd->qhd", probs_low, value_heads, preferred_element_type=jnp.float32)
            .reshape(local, width)
            .astype(jnp.bfloat16)
        )
        pre = source.astype(jnp.float32) + matmul(mixed, params[5]) + params[6].astype(jnp.float32)
        first, first_back = jax.vjp(
            layer_norm, pre, params[7].astype(jnp.float32), params[8].astype(jnp.float32)
        )
        first_low = first.astype(jnp.bfloat16)
        inner = matmul(first_low, params[9]) + params[10].astype(jnp.float32)
        active, gelu_back = jax.vjp(gelu_exact, inner)
        active_low = active.astype(jnp.bfloat16)
        total = first + matmul(active_low, params[11]) + params[12].astype(jnp.float32)
        result, second_back = jax.vjp(
            layer_norm, total, params[13].astype(jnp.float32), params[14].astype(jnp.float32)
        )
        outputs.append(result.astype(jnp.bfloat16))
        later = (
            lax.all_gather(shards[0], ("dp", "ctx"), axis=0, tiled=True),
            lax.all_gather(shards[1], ("dp", "ctx"), axis=0, tiled=True),
            lax.all_gather(shards[2], ("dp", "ctx"), axis=0, tiled=True),
            lax.all_gather(shards[3], ("dp", "ctx"), axis=0, tiled=True),
            lax.all_gather(shards[4], ("dp", "ctx"), axis=0, tiled=True),
            lax.all_gather(shards[5], ("dp", "ctx"), axis=0, tiled=True),
            lax.all_gather(shards[6], ("dp", "ctx"), axis=0, tiled=True),
            lax.all_gather(shards[7], ("dp", "ctx"), axis=0, tiled=True),
            lax.all_gather(shards[8], ("dp", "ctx"), axis=0, tiled=True),
            lax.all_gather(shards[9], ("dp", "ctx"), axis=0, tiled=True),
            lax.all_gather(shards[10], ("dp", "ctx"), axis=0, tiled=True),
            lax.all_gather(shards[11], ("dp", "ctx"), axis=0, tiled=True),
            lax.all_gather(shards[12], ("dp", "ctx"), axis=0, tiled=True),
            lax.all_gather(shards[13], ("dp", "ctx"), axis=0, tiled=True),
            lax.all_gather(shards[14], ("dp", "ctx"), axis=0, tiled=True),
        )
        d_total, d_second_gain, d_second_shift = second_back(
            cotangent[micro_step].astype(jnp.float32)
        )
        d_outer = d_total.astype(jnp.bfloat16)
        g_outer_weight = jnp.einsum(
            "tf,td->fd", active_low, d_outer, preferred_element_type=jnp.float32
        )
        g_outer_bias = column_sums(d_outer)
        d_active = jnp.einsum("td,fd->tf", d_outer, later[11], preferred_element_type=jnp.float32)
        d_inner = gelu_back(d_active)[0].astype(jnp.bfloat16)
        g_inner_weight = jnp.einsum(
            "td,tf->df", first_low, d_inner, preferred_element_type=jnp.float32
        )
        g_inner_bias = column_sums(d_inner)
        d_first = (
            jnp.einsum("tf,df->td", d_inner, later[9], preferred_element_type=jnp.float32) + d_total
        )
        d_pre, d_first_gain, d_first_shift = first_back(d_first)
        d_attended = d_pre.astype(jnp.bfloat16)
        g_output_weight = jnp.einsum(
            "td,te->de", mixed, d_attended, preferred_element_type=jnp.float32
        )
        g_output_bias = column_sums(d_attended)
        d_mixed = (
            jnp.einsum("te,de->td", d_attended, later[5], preferred_element_type=jnp.float32)
            .astype(jnp.bfloat16)
            .reshape(local, HEADS, HEAD)
        )
        again = masked_scores(query_heads, key_heads, allowed, scale)
        probs = jnp.exp(again - logsum)
        d_probs = jnp.einsum(
            "qhd,khd->hqk", d_mixed, value_heads, preferred_element_type=jnp.float32
        )
        row_sums = jnp.sum(probs * d_probs, axis=-1, keepdims=True)
        d_scores = (probs * (d_probs - row_sums)).astype(jnp.bfloat16)
        d_queries = (
            (
                jnp.einsum("hqk,khd->qhd", d_scores, key_heads, preferred_element_type=jnp.float32)
                * scale
            )
            .reshape(local, width)
            .astype(jnp.bfloat16)
        )
        probs_low = probs.astype(jnp.bfloat16)
        key_terms = (
            jnp.einsum("hqk,qhd->khd", d_scores, query_heads, preferred_element_type=jnp.float32)
            * scale
        ).reshape(-1, width)
        value_terms = jnp.einsum(
            "hqk,qhd->khd", probs_low, d_mixed, preferred_element_type=jnp.float32
        ).reshape(-1, width)
        d_keys, d_values = (
            lax.psum_scatter(
                key_terms.astype(jnp.bfloat16), "ctx", scatter_dimension=0, tiled=True
            ).astype(jnp.float32),
            lax.psum_scatter(
                value_terms.astype(jnp.bfloat16), "ctx", scatter_dimension=0, tiled=True
            ).astype(jnp.float32),
        )
        d_keys = d_keys.astype(jnp.bfloat16)
        d_values = d_values.astype(jnp.bfloat16)
        g_query_weight = jnp.einsum(
            "td,te->de", source, d_queries, preferred_element_type=jnp.float32
        )
        g_query_bias = column_sums(d_queries)
        g_key_weight = jnp.einsum("td,te->de", source, d_keys, preferred_element_type=jnp.float32)
        g_value_weight = jnp.einsum(
            "td,te->de", source, d_values, preferred_element_type=jnp.float32
        )
        g_value_bias = column_sums(d_values)
        d_input = d_pre + jnp.einsum(
            "te,de->td", d_queries, later[0], preferred_element_type=jnp.float32
        )
        d_input = d_input + jnp.einsum(
            "te,de->td", d_keys, later[2], preferred_element_type=jnp.float32
        )
        d_input = d_input + jnp.einsum(
            "te,de->td", d_values, later[3], preferred_element_type=jnp.float32
        )
        input_grads.append(d_input)
        local_grads = (
            g_query_weight,
            g_query_bias,
            g_key_weight,
            g_value_weight,
            g_value_bias,
            g_output_weight,
            g_output_bias,
            d_first_gain,
            d_first_shift,
            g_inner_weight,
            g_inner_bias,
            g_outer_weight,
            g_outer_bias,
            d_second_gain,
            d_second_shift,
        )
        totals = local_grads if totals is None else jax.tree.map(jnp.add, totals, local_grads)
    owned = lax.psum_scatter(totals, ("dp", "ctx"), scatter_dimension=0, tiled=True)
    return (
        jnp.stack(outputs),
        jnp.stack(input_grads),
        owned[0],
        owned[1],
        owned[2],
        owned[3],
        owned[4],
        owned[5],
        owned[6],
        owned[7],
        owned[8],
        owned[9],
        owned[10],
        owned[11],
        owned[12],
        owned[13],
        owned[14],
    )


def solution(mesh):
    return jax.shard_map(
        on_device,
        mesh=mesh,
        in_specs=(
            P("dp", "ctx", None),
            P("dp", None),
            P("dp", "ctx", None),
            P(("dp", "ctx"), None),
            P(("dp", "ctx")),
            P(("dp", "ctx"), None),
            P(("dp", "ctx"), None),
            P(("dp", "ctx")),
            P(("dp", "ctx"), None),
            P(("dp", "ctx")),
            P(("dp", "ctx")),
            P(("dp", "ctx")),
            P(("dp", "ctx"), None),
            P(("dp", "ctx")),
            P(("dp", "ctx"), None),
            P(("dp", "ctx")),
            P(("dp", "ctx")),
            P(("dp", "ctx")),
        ),
        out_specs=(
            P("dp", "ctx", None),
            P("dp", "ctx", None),
            P(("dp", "ctx"), None),
            P(("dp", "ctx")),
            P(("dp", "ctx"), None),
            P(("dp", "ctx"), None),
            P(("dp", "ctx")),
            P(("dp", "ctx"), None),
            P(("dp", "ctx")),
            P(("dp", "ctx")),
            P(("dp", "ctx")),
            P(("dp", "ctx"), None),
            P(("dp", "ctx")),
            P(("dp", "ctx"), None),
            P(("dp", "ctx")),
            P(("dp", "ctx")),
            P(("dp", "ctx")),
        ),
        check_vma=False,
    )
```

profile of v0, /device:TPU:0, one launch (start us, length us, event | category | flops | bytes accessed | tf_op | source)
XLA Modules:
  0.0 1531.9 jit_solution(13532980301998678464)
XLA Ops:
  9.6 58.2 %all-gather.17.cloned.1.call-done = bf16[768,768]{1,0:T(8,128)(2,1)} async-done(((bf16[24,768]{1,0:T(8,128)(2,1)}), bf16[768,768]{1,0:T(8,128)(2,1)}) %all-gather.17.cloned.1.call-update) | async-done | bytes 1179664 | tf_op jit(solution)/shard_map/all_gather | solution.py:27
  73.2 39.7 %all-reduce.19 = (bf16[768]{0:T(1024)(128)(2,1)S(1)}, bf16[768]{0:T(1024)(128)(2,1)S(1)}, bf16[768]{0:T(1024)(128)(2,1)S(1)}, bf16[768]{0:T(1024)(128)(2,1)S(1)}...) all-reduce(bf16[768]{0:T(1024)(128)(2,1)S(1)} %dynamic-update-slice, ...), channel_id=1, replica_groups=mesh['dp'=8,'ctx'=4] {'dp','ctx'}, use_global_device_ids=true, to_apply=%add | all-reduce | flops 9216 | bytes 36864
  112.9 10.7 all-gather.11.cloned.1.call-done
  136.6 42.9 %all-gather.15.cloned.1.call-done = bf16[768,768]{1,0:T(8,128)(2,1)} async-done(((bf16[24,768]{1,0:T(8,128)(2,1)}), bf16[768,768]{1,0:T(8,128)(2,1)}) %all-gather.15.cloned.1.call-update) | async-done | bytes 1179664 | tf_op jit(solution)/shard_map/all_gather | solution.py:25
  190.2 18.2 %all-gather.29.cloned.1.call-done = bf16[2048,768]{1,0:T(8,128)(2,1)} async-done(((bf16[512,768]{1,0:T(8,128)(2,1)}), bf16[2048,768]{1,0:T(8,128)(2,1)}) %all-gather.29.cloned.1.call-update) | async-done | bytes 3145744 | tf_op jit(solution)/shard_map/all_gather | solution.py:116
  208.4 4.8 copy.70
  213.2 22.5 %fusion.1 = (f32[12,512]{1,0:T(8,128)S(1)}, f32[12,512,2048]{2,1,0:T(8,128)}) fusion(pred[512,2048]{1,0:T(8,128)(4,1)S(1)} %broadcast_compare_fusion, bf16[512,12,64]{0,2,1:T(8,128)(2,1)S(1)} %bitcast.203, bf16[2048,12,64]{0,2,1:T(8,128)(2,1)} %bitcast.193), kind=kOutput, calls=%fused_computation.11 | convolution fusion | flops 1648355328 | bytes 55336960 | tf_op jit(solution)/shard_map/qhd,khd->hqk/dot_general | solution.py:45
  235.7 21.9 %exponential_reduce_fusion = f32[12,512]{1,0:T(8,128)S(1)} fusion(f32[12,512,2048]{2,1,0:T(8,128)} %get-tuple-element.145, f32[12,512]{1,0:T(8,128)S(1)} %get-tuple-element.144, pred[512,2048]{1,0:T(8,128)(4,1)S(1)} %broadcast_compare_fusion), kind=kLoop, calls=%fused_computation.5 | loop fusion | flops 50325504 | bytes 51429376 | tf_op jit(solution)/shard_map/reduce_sum | solution.py:124
  257.7 4.6 copy.68
  262.3 20.3 %convolution_convert_fusion.2 = bf16[12,64,512]{2,1,0:T(8,128)(2,1)S(1)} fusion(bf16[2048,12,64]{0,2,1:T(8,128)(2,1)} %bitcast.197, f32[12,512,2048]{2,1,0:T(8,128)} %get-tuple-element.145, f32[12,512]{1,0:T(8,128)S(1)} %log_add_fusion, pred[512,2048]{1,0:T(8,128)(4,1)S(1)} %broadcast_compare_fusion), kind=kOutput, calls=%fused_computation.122 | convolution fusion | flops 1661337600 | bytes 55336960 | tf_op jit(solution)/shard_map/hqk,khd->qhd/dot_general | solution.py:127
  282.6 13.1 all-gather.21.cloned.1.call-done
  299.1 25.5 %all-gather.19.cloned.1.call-done = bf16[2048,768]{1,0:T(8,128)(2,1)} async-done(((bf16[512,768]{1,0:T(8,128)(2,1)}), bf16[2048,768]{1,0:T(8,128)(2,1)}) %all-gather.19.cloned.1.call-update) | async-done | bytes 3145744 | tf_op jit(solution)/shard_map/all_gather | solution.py:116
  324.7 4.7 copy.67
  329.4 22.7 %fusion = (f32[12,512]{1,0:T(8,128)S(1)}, f32[12,512,2048]{2,1,0:T(8,128)}) fusion(pred[512,2048]{1,0:T(8,128)(4,1)S(1)} %broadcast_compare_fusion.1, bf16[512,12,64]{0,2,1:T(8,128)(2,1)S(1)} %bitcast.205, bf16[2048,12,64]{0,2,1:T(8,128)(2,1)} %bitcast.195), kind=kOutput, calls=%fused_computation.10 | convolution fusion | flops 1648355328 | bytes 55336960 | tf_op jit(solution)/shard_map/qhd,khd->hqk/dot_general | solution.py:45
  352.1 22.0 %exponential_reduce_fusion.1 = f32[12,512]{1,0:T(8,128)S(1)} fusion(f32[12,512,2048]{2,1,0:T(8,128)} %get-tuple-element.141, f32[12,512]{1,0:T(8,128)S(1)} %get-tuple-element.140, pred[512,2048]{1,0:T(8,128)(4,1)S(1)} %broadcast_compare_fusion.1), kind=kLoop, calls=%fused_computation.8 | loop fusion | flops 50325504 | bytes 51429376 | tf_op jit(solution)/shard_map/reduce_sum | solution.py:124
  374.2 4.7 copy.65
  378.9 20.7 %convolution_convert_fusion.3 = bf16[12,64,512]{2,1,0:T(8,128)(2,1)S(1)} fusion(bf16[2048,12,64]{0,2,1:T(8,128)(2,1)} %bitcast.199, f32[12,512,2048]{2,1,0:T(8,128)} %get-tuple-element.141, f32[12,512]{1,0:T(8,128)S(1)} %log_add_fusion.1, pred[512,2048]{1,0:T(8,128)(4,1)S(1)} %broadcast_compare_fusion.1), kind=kOutput, calls=%fused_computation.123 | convolution fusion | flops 1661337600 | bytes 55336960 | tf_op jit(solution)/shard_map/hqk,khd->qhd/dot_general | solution.py:127
  402.0 19.2 %all-gather.23.cloned.1.call-done = bf16[768,3072]{1,0:T(8,128)(2,1)} async-done(((bf16[24,3072]{1,0:T(8,128)(2,1)}), bf16[768,3072]{1,0:T(8,128)(2,1)}) %all-gather.23.cloned.1.call-update) | async-done | bytes 4718608 | tf_op jit(solution)/shard_map/all_gather | solution.py:34
  421.3 5.3 fusion.76
  429.2 35.1 %multiply_convert_fusion.5 = (bf16[512,3072]{1,0:T(8,128)(2,1)}, f32[512,3072]{1,0:T(8,128)}, bf16[512,3072]{1,0:T(8,128)(2,1)}, f32[512,3072]{1,0:T(8,128)}, f32[512,3072]{1,0:T(8,128)}) fusion(f32[3072]{0:T(1024)S(1)} %convert_element_type.260, f32[512,3072]{1,0:T(8,128)S(1)} %fusion.76, bf16[768,3072]{1,0:T(8,128)(2,1)S(1)} %copy-done.85, ...), kind=kOutput, calls=%fused_computation.37 | convolution fusion | flops 2625503232 | bytes 37771264 | tf_op jit(solution)/shard_map/dot_general | solution.py:52
  464.3 21.6 %all-gather.25.cloned.1.call-done = bf16[3072,768]{1,0:T(8,128)(2,1)} async-done(((bf16[96,768]{1,0:T(8,128)(2,1)}), bf16[3072,768]{1,0:T(8,128)(2,1)}) %all-gather.25.cloned.1.call-update) | async-done | bytes 4718608 | tf_op jit(solution)/shard_map/all_gather | solution.py:36
  485.9 6.6 fusion.91
  503.3 4.7 fusion.95
  508.0 17.7 %convert_reduce_fusion.1 = (f32[3072]{0:T(1024)}, bf16[512,3072]{1,0:T(8,128)(2,1)}, f32[3072]{0:T(1024)}, bf16[512,3072]{1,0:T(8,128)(2,1)}) fusion(f32[512,3072]{1,0:T(8,128)} %get-tuple-element.121, f32[512,3072]{1,0:T(8,128)} %get-tuple-element.148, f32[3072]{0:T(1024)S(1)} %convert_element_type.260, f32[512,3072]{1,0:T(8,128)} %fusion.95, ...), kind=kOutput, calls=%fused_computation.19 | convolution fusion | flops 2469390336 | bytes 43290624 | tf_op jit(solution)/shard_map/td,fd->tf/dot_general | solution.py:169
  525.7 6.5 add_add_fusion.8
  532.2 6.4 multiply_reduce_fusion.3
  544.8 22.6 %convolution_convert_fusion.1 = bf16[12,64,2048]{2,1,0:T(8,128)(2,1)} fusion(bf16[512,12,64]{0,2,1:T(8,128)(2,1)S(1)} %bitcast.213, f32[12,512,2048]{2,1,0:T(8,128)} %get-tuple-element.141, f32[12,512]{1,0:T(8,128)S(1)} %log_add_fusion.1, pred[512,2048]{1,0:T(8,128)(4,1)S(1)} %broadcast_compare_fusion.1), kind=kOutput, calls=%fused_computation.55 | convolution fusion | flops 1662517248 | bytes 55336960 | tf_op jit(solution)/shard_map/hqk,qhd->khd/dot_general | solution.py:209
  575.5 22.9 %convolution_convert_fusion = bf16[12,64,2048]{2,1,0:T(8,128)(2,1)} fusion(bf16[512,12,64]{0,2,1:T(8,128)(2,1)S(1)} %bitcast.211, f32[12,512,2048]{2,1,0:T(8,128)} %get-tuple-element.145, f32[12,512]{1,0:T(8,128)S(1)} %copy-done.52, pred[512,2048]{1,0:T(8,128)(4,1)S(1)} %copy-done.1), kind=kOutput, calls=%fused_computation.54 | convolution fusion | flops 1662517248 | bytes 55336960 | tf_op jit(solution)/shard_map/hqk,qhd->khd/dot_general | solution.py:209
  599.5 38.1 %multiply_reduce_fusion.1 = (f32[12,512]{1,0:T(8,128)S(1)}, f32[12,512,2048]{2,1,0:T(8,128)}) fusion(f32[12,512,2048]{2,1,0:T(8,128)} %get-tuple-element.141, f32[12,512]{1,0:T(8,128)S(1)} %log_add_fusion.1, pred[512,2048]{1,0:T(8,128)(4,1)S(1)} %broadcast_compare_fusion.1, bf16[512,12,64]{0,2,1:T(8,128)(2,1)S(1)} %bitcast.214, ...), kind=kOutput, calls=%fused_computation.3 | convolution fusion | flops 1673521152 | bytes 105693184 | tf_op jit(solution)/shard_map/qhd,khd->hqk/dot_general | solution.py:191
  637.6 40.5 %multiply_convert_fusion.1 = bf16[12,512,2048]{2,1,0:T(8,128)(2,1)} fusion(f32[12,512,2048]{2,1,0:T(8,128)} %get-tuple-element.157, f32[12,512,2048]{2,1,0:T(8,128)} %get-tuple-element.141, f32[12,512]{1,0:T(8,128)S(1)} %get-tuple-element.156, f32[12,512]{1,0:T(8,128)S(1)} %log_add_fusion.1, pred[512,2048]{1,0:T(8,128)(4,1)S(1)} %broadcast_compare_fusion.1), kind=kLoop, calls=%fused_computation.2 | loop fusion | flops 75497472 | bytes 126926848 | tf_op jit(solution)/shard_map/convert_element_type | solution.py:195
  678.2 14.3 multiply_convert_fusion.3
  693.6 38.4 %multiply_reduce_fusion = (f32[12,512]{1,0:T(8,128)S(1)}, f32[12,512,2048]{2,1,0:T(8,128)}) fusion(f32[12,512,2048]{2,1,0:T(8,128)} %get-tuple-element.145, f32[12,512]{1,0:T(8,128)S(1)} %copy-done.52, pred[512,2048]{1,0:T(8,128)(4,1)S(1)} %copy-done.1, bf16[512,12,64]{0,2,1:T(8,128)(2,1)S(1)} %bitcast.212, bf16[2048,12,64]{0,2,1:T(8,128)(2,1)} %bitcast.198), kind=kOutput, calls=%fused_computation.1 | convolution fusion | flops 1673521152 | bytes 105693184 | tf_op jit(solution)/shard_map/qhd,khd->hqk/dot_general | solution.py:191
  731.9 40.4 %multiply_convert_fusion = bf16[12,512,2048]{2,1,0:T(8,128)(2,1)} fusion(f32[12,512,2048]{2,1,0:T(8,128)} %get-tuple-element.155, f32[12,512,2048]{2,1,0:T(8,128)} %get-tuple-element.145, f32[12,512]{1,0:T(8,128)S(1)} %get-tuple-element.154, f32[12,512]{1,0:T(8,128)S(1)} %copy-done.52, pred[512,2048]{1,0:T(8,128)(4,1)S(1)} %copy-done.1), kind=kLoop, calls=%fused_computation | loop fusion | flops 75497472 | bytes 126926848 | tf_op jit(solution)/shard_map/convert_element_type | solution.py:195
  772.4 14.3 multiply_convert_fusion.2
  792.7 14.3 convert_reduce_fusion.11
  810.7 13.6 convert_reduce_fusion.10
  824.3 4.3 add_bitcast_fusion.2
  835.3 4.2 add_bitcast_fusion
  853.9 5.0 fusion.78
  858.9 5.8 convolution_add_fusion.1
  864.9 5.0 fusion.99
  869.9 5.3 convolution_add_fusion
  883.0 40.9 %all-reduce.18 = (f32[768]{0:T(1024)S(1)}, f32[768]{0:T(1024)S(1)}, f32[768]{0:T(1024)S(1)}, f32[768]{0:T(1024)S(1)}, f32[768]{0:T(1024)S(1)}, /*index=5*/f32[30...) all-reduce(f32[768]{0:T(1024)S(1)} %add.332, ...), channel_id=7, replica_groups=mesh['dp'=8,'ctx'=4] {'dp','ctx'}, use_global_device_ids=true, to_apply=%region_29.30.clone | all-reduce | flops 9216 | bytes 73728
  937.0 96.0 %reduce-scatter.31.cloned.1.call-done = f32[24,768]{1,0:T(8,128)} async-done(((f32[768,768]{1,0:T(8,128)}), f32[24,768]{1,0:T(8,128)}) %reduce-scatter.31.cloned.1.call-update) | async-done | bytes 73744
  1033.0 104.4 %reduce-scatter.35.cloned.1.call-done = f32[24,768]{1,0:T(8,128)} async-done(((f32[768,768]{1,0:T(8,128)}), f32[24,768]{1,0:T(8,128)}) %reduce-scatter.35.cloned.1.call-update) | async-done | bytes 73744
  1137.3 104.3 %reduce-scatter.33.cloned.1.call-done = f32[24,768]{1,0:T(8,128)} async-done(((f32[768,768]{1,0:T(8,128)}), f32[24,768]{1,0:T(8,128)}) %reduce-scatter.33.cloned.1.call-update) | async-done | bytes 73744
  1241.6 141.8 %reduce-scatter.27.cloned.1.call-done = f32[24,3072]{1,0:T(8,128)} async-done(((f32[768,3072]{1,0:T(8,128)}), f32[24,3072]{1,0:T(8,128)}) %reduce-scatter.27.cloned.1.call-update) | async-done | bytes 294928 | tf_op jit(solution)/shard_map/reduce_scatter | solution.py:259
  1383.4 141.4 %reduce-scatter.29.cloned.1.call-done = f32[96,768]{1,0:T(8,128)} async-done(((f32[3072,768]{1,0:T(8,128)}), f32[96,768]{1,0:T(8,128)}) %reduce-scatter.29.cloned.1.call-update) | async-done | bytes 294928 | tf_op jit(solution)/shard_map/reduce_scatter | solution.py:259
  (365 shorter events, 117.8 us)
Async XLA Ops:
  7.2 116.4 %copy-start.7 = (bf16[2,512,768]{2,1,0:T(8,128)(2,1)S(1)}, bf16[2,512,768]{2,1,0:T(8,128)(2,1)}, u32[]{:S(2)}) copy-start(bf16[2,512,768]{2,1,0:T(8,128)(2,1)} %param.18) | copy-start | bytes 4718596
  7.2 63.9 %copy-start.91 = (bf16[24]{0:T(256)(128)(2,1)S(1)}, bf16[24]{0:T(256)(128)(2,1)}, u32[]{:S(2)}) copy-start(bf16[24]{0:T(256)(128)(2,1)} %param.35) | copy-start | bytes 148
  7.2 64.1 %copy-start.92 = (bf16[24]{0:T(256)(128)(2,1)S(1)}, bf16[24]{0:T(256)(128)(2,1)}, u32[]{:S(2)}) copy-start(bf16[24]{0:T(256)(128)(2,1)} %param.33) | copy-start | bytes 148
  7.2 64.3 %copy-start.93 = (bf16[24]{0:T(256)(128)(2,1)S(1)}, bf16[24]{0:T(256)(128)(2,1)}, u32[]{:S(2)}) copy-start(bf16[24]{0:T(256)(128)(2,1)} %param.28) | copy-start | bytes 148
  7.2 64.6 %copy-start.94 = (bf16[24]{0:T(256)(128)(2,1)S(1)}, bf16[24]{0:T(256)(128)(2,1)}, u32[]{:S(2)}) copy-start(bf16[24]{0:T(256)(128)(2,1)} %param.29) | copy-start | bytes 148
  7.2 64.8 %copy-start.95 = (bf16[24]{0:T(256)(128)(2,1)S(1)}, bf16[24]{0:T(256)(128)(2,1)}, u32[]{:S(2)}) copy-start(bf16[24]{0:T(256)(128)(2,1)} %param.27) | copy-start | bytes 148
  7.3 65.0 %copy-start.96 = (bf16[24]{0:T(256)(128)(2,1)S(1)}, bf16[24]{0:T(256)(128)(2,1)}, u32[]{:S(2)}) copy-start(bf16[24]{0:T(256)(128)(2,1)} %param.22) | copy-start | bytes 148
  7.3 65.2 %copy-start.97 = (bf16[24]{0:T(256)(128)(2,1)S(1)}, bf16[24]{0:T(256)(128)(2,1)}, u32[]{:S(2)}) copy-start(bf16[24]{0:T(256)(128)(2,1)} %param.25) | copy-start | bytes 148
  7.3 65.5 %copy-start.98 = (bf16[24]{0:T(256)(128)(2,1)S(1)}, bf16[24]{0:T(256)(128)(2,1)}, u32[]{:S(2)}) copy-start(bf16[24]{0:T(256)(128)(2,1)} %param.34) | copy-start | bytes 148
  7.3 65.7 %copy-start.99 = (bf16[96]{0:T(256)(128)(2,1)S(1)}, bf16[96]{0:T(256)(128)(2,1)}, u32[]{:S(2)}) copy-start(bf16[96]{0:T(256)(128)(2,1)} %param.31) | copy-start | bytes 580
  7.3 60.4 %all-gather.17.cloned.1.call-start = ((), (), s32[]{:S(2)}) async-start(), calls=%async_computation.13 | async-start | bytes 1216512 | tf_op jit(solution)/shard_map/all_gather | solution.py:27
  8.0 115.6 %all-gather.11.cloned.1.call-start = ((), (), s32[]{:S(2)}) async-start(), calls=%async_computation.10 | async-start | bytes 1216512 | tf_op jit(solution)/shard_map/all_gather | solution.py:28
  8.8 170.7 %all-gather.15.cloned.1.call-start = ((), (), s32[]{:S(2)}) async-start(), calls=%async_computation.12 | async-start | bytes 1216512 | tf_op jit(solution)/shard_map/all_gather | solution.py:25
  9.5 198.9 %all-gather.29.cloned.1.call-start = ((), (), s32[]{:S(2)}) async-start(), calls=%async_computation.19 | async-start | bytes 3932160 | tf_op jit(solution)/shard_map/all_gather | solution.py:116
  71.0 186.7 %all-gather.27.cloned.1.call-start = ((), (), s32[]{:S(2)}) async-start(), calls=%async_computation.18 | async-start | bytes 3932160 | tf_op jit(solution)/shard_map/all_gather | solution.py:117
  126.6 169.1 %all-gather.21.cloned.1.call-start = ((), (), s32[]{:S(2)}) async-start(), calls=%async_computation.15 | async-start | bytes 1216512 | tf_op jit(solution)/shard_map/all_gather | solution.py:30
  127.2 197.5 %all-gather.19.cloned.1.call-start = ((), (), s32[]{:S(2)}) async-start(), calls=%async_computation.14 | async-start | bytes 3932160 | tf_op jit(solution)/shard_map/all_gather | solution.py:116
  130.2 243.9 %all-gather.13.cloned.1.call-start = ((), (), s32[]{:S(2)}) async-start(), calls=%async_computation.11 | async-start | bytes 3932160 | tf_op jit(solution)/shard_map/all_gather | solution.py:117
  132.0 289.3 %all-gather.23.cloned.1.call-start = ((), (), s32[]{:S(2)}) async-start(), calls=%async_computation.16 | async-start | bytes 4866048 | tf_op jit(solution)/shard_map/all_gather | solution.py:34
  132.7 353.2 %all-gather.25.cloned.1.call-start = ((), (), s32[]{:S(2)}) async-start(), calls=%async_computation.17 | async-start | bytes 4866048 | tf_op jit(solution)/shard_map/all_gather | solution.py:36
  133.3 698.6 %reduce-scatter.19.cloned.1.call-start = ((), (), s32[]{:S(2)}) async-start(), calls=%async_computation.21 | async-start | bytes 3932160 | tf_op jit(solution)/shard_map/reduce_scatter | solution.py:216
  133.4 405.3 %copy-start.53 = (f32[768]{0:T(1024)}, f32[768]{0:T(1024)S(1)}, u32[]{:S(2)}) copy-start(f32[768]{0:T(1024)S(1)} %convert_element_type.257) | copy-start | bytes 9220
  133.4 359.5 %copy-start.55 = (f32[768]{0:T(1024)}, f32[768]{0:T(1024)S(1)}, u32[]{:S(2)}) copy-start(f32[768]{0:T(1024)S(1)} %convert_element_type.258) | copy-start | bytes 9220
  136.6 125.8 %copy-start = (pred[512,2048]{1,0:T(8,128)(4,1)}, pred[512,2048]{1,0:T(8,128)(4,1)S(1)}, u32[]{:S(2)}) copy-start(pred[512,2048]{1,0:T(8,128)(4,1)S(1)} %broadcast_compare_fusion) | copy-start | bytes 3145732
  184.1 29.1 %copy-start.15 = (bf16[512,768]{0,1:T(8,128)(2,1)}, bf16[512,768]{0,1:T(8,128)(2,1)S(1)}, u32[]{:S(2)}) copy-start(bf16[512,768]{0,1:T(8,128)(2,1)S(1)} %copy.69) | copy-start | bytes 2359300
  282.6 46.8 %copy-start.46 = (bf16[12,64,512]{2,1,0:T(8,128)(2,1)}, bf16[12,64,512]{2,1,0:T(8,128)(2,1)S(1)}, u32[]{:S(2)}) copy-start(bf16[12,64,512]{2,1,0:T(8,128)(2,1)S(1)} %convolution_convert_fusion.2) | copy-start | bytes 2359300
  299.1 239.6 %copy-start.57 = (f32[512]{0:T(512)}, f32[512]{0:T(512)S(1)}, u32[]{:S(2)}) copy-start(f32[512]{0:T(512)S(1)} %broadcast_multiply_fusion.1) | copy-start | bytes 6148
  299.1 30.3 %copy-start.17 = (bf16[512,768]{0,1:T(8,128)(2,1)S(1)}, bf16[512,768]{0,1:T(8,128)(2,1)}, u32[]{:S(2)}) copy-start(bf16[512,768]{0,1:T(8,128)(2,1)} %copy.66) | copy-start | bytes 2359300
  378.9 20.7 %copy-start.8 = (bf16[2,512,768]{2,1,0:T(8,128)(2,1)S(1)}, bf16[2,512,768]{2,1,0:T(8,128)(2,1)}, u32[]{:S(2)}) copy-start(bf16[2,512,768]{2,1,0:T(8,128)(2,1)} %param.18) | copy-start | bytes 4718596
  378.9 20.7 %copy-start.89 = (bf16[768,768]{1,0:T(8,128)(2,1)S(1)}, bf16[768,768]{1,0:T(8,128)(2,1)}, u32[]{:S(2)}) copy-start(bf16[768,768]{1,0:T(8,128)(2,1)} %all-gather.21.cloned.1.call-done) | copy-start | bytes 3538948
  400.5 138.2 %copy-start.62 = (f32[512]{0:T(512)}, f32[512]{0:T(512)S(1)}, u32[]{:S(2)}) copy-start(f32[512]{0:T(512)S(1)} %broadcast_multiply_fusion.3) | copy-start | bytes 6148
  402.0 136.7 %copy-start.60 = (f32[512]{0:T(512)}, f32[512]{0:T(512)S(1)}, u32[]{:S(2)}) copy-start(f32[512]{0:T(512)S(1)} %fusion.65) | copy-start | bytes 6148
  402.0 136.7 %copy-start.78 = (f32[512]{0:T(512)}, f32[512]{0:T(512)S(1)}, u32[]{:S(2)}) copy-start(f32[512]{0:T(512)S(1)} %fusion.63) | copy-start | bytes 6148
  421.3 8.0 copy-start.85
  429.2 56.7 %copy-start.84 = (f32[768]{0:T(1024)S(1)}, f32[768]{0:T(1024)}, u32[]{:S(2)}) copy-start(f32[768]{0:T(1024)} %convert_element_type.262) | copy-start | bytes 9220
  544.8 22.6 %copy-start.36 = (bf16[512,768]{0,1:T(8,128)(2,1)}, bf16[512,768]{0,1:T(8,128)(2,1)S(1)}, u32[]{:S(2)}) copy-start(bf16[512,768]{0,1:T(8,128)(2,1)S(1)} %copy.71) | copy-start | bytes 2359300
  567.5 267.8 %reduce-scatter.23.cloned.1.call-start = ((), (), s32[]{:S(2)}) async-start(), calls=%async_computation.23 | async-start | bytes 3932160 | tf_op jit(solution)/shard_map/reduce_scatter | solution.py:216
  575.5 23.0 %copy-start.34 = (bf16[512,768]{0,1:T(8,128)(2,1)}, bf16[512,768]{0,1:T(8,128)(2,1)S(1)}, u32[]{:S(2)}) copy-start(bf16[512,768]{0,1:T(8,128)(2,1)S(1)} %copy.72) | copy-start | bytes 2359300
  598.4 244.2 %reduce-scatter.17.cloned.1.call-start = ((), (), s32[]{:S(2)}) async-start(), calls=%async_computation.20 | async-start | bytes 3932160 | tf_op jit(solution)/shard_map/reduce_scatter | solution.py:213
  637.6 40.5 %copy-start.18 = (bf16[512,768]{0,1:T(8,128)(2,1)S(1)}, bf16[512,768]{0,1:T(8,128)(2,1)}, u32[]{:S(2)}) copy-start(bf16[512,768]{0,1:T(8,128)(2,1)} %copy.66) | copy-start | bytes 2359300
  692.5 153.5 %reduce-scatter.21.cloned.1.call-start = ((), (), s32[]{:S(2)}) async-start(), calls=%async_computation.22 | async-start | bytes 3932160 | tf_op jit(solution)/shard_map/reduce_scatter | solution.py:213
  731.9 40.4 %copy-start.16 = (bf16[512,768]{0,1:T(8,128)(2,1)S(1)}, bf16[512,768]{0,1:T(8,128)(2,1)}, u32[]{:S(2)}) copy-start(bf16[512,768]{0,1:T(8,128)(2,1)} %copy-done.15) | copy-start | bytes 2359300
  786.7 150.3 %reduce-scatter.25.cloned.1.call-start = ((), (), s32[]{:S(2)}) async-start(), calls=%async_computation.24 | async-start | bytes 2433024 | tf_op jit(solution)/shard_map/reduce_scatter | solution.py:259
  792.6 240.4 %reduce-scatter.31.cloned.1.call-start = ((), (), s32[]{:S(2)}) async-start(), calls=%async_computation.27 | async-start | bytes 2433024
  831.9 305.5 %reduce-scatter.35.cloned.1.call-start = ((), (), s32[]{:S(2)}) async-start(), calls=%async_computation.29 | async-start | bytes 2433024
  842.6 399.0 %reduce-scatter.33.cloned.1.call-start = ((), (), s32[]{:S(2)}) async-start(), calls=%async_computation.28 | async-start | bytes 2433024
  853.4 530.1 %reduce-scatter.27.cloned.1.call-start = ((), (), s32[]{:S(2)}) async-start(), calls=%async_computation.25 | async-start | bytes 9732096 | tf_op jit(solution)/shard_map/reduce_scatter | solution.py:259
  864.8 660.1 %reduce-scatter.29.cloned.1.call-start = ((), (), s32[]{:S(2)}) async-start(), calls=%async_computation.26 | async-start | bytes 9732096 | tf_op jit(solution)/shard_map/reduce_scatter | solution.py:259
  (74 other events, 252.9 us)
Sparse Core Ops, SparseCore 0:
  11.0 56.6 all-gather.16
  70.6 52.9 all-gather.10
  126.5 52.9 all-gather.14
  180.9 27.4 all-gather.28
  210.4 28.4 all-gather.26
  241.7 53.9 all-gather.20
  297.2 27.4 all-gather.18
  326.2 28.4 all-gather.12
  357.7 63.5 all-gather.22
  424.0 61.8 all-gather.24
  567.6 36.0 reduce-scatter.18
  606.1 37.7 reduce-scatter.22
  692.6 36.9 reduce-scatter.16
  786.8 36.1 reduce-scatter.20
  828.8 99.8 reduce-scatter.24
  934.4 98.5 reduce-scatter.30
  1038.7 98.6 reduce-scatter.34
  1143.0 98.5 reduce-scatter.32
  1248.1 135.2 reduce-scatter.26
  1389.8 135.0 reduce-scatter.28
where the time goes:
time: 1540 us; the launch traced here: 1530 us
  waiting for transfers between devices  801 us (52%)
  matrix products  433 us (28%)
  other arithmetic  145 us (9%)
  blocking collectives  80.6 us (5%)
  local copies, waits for them, and re-layouts  54.7 us (4%)
  between operations  15.9 us (1%)
    unnamed x23, waiting for transfers between devices  309 us
    reduce_scatter x3, waiting for transfers between devices, on_device(): lax.psum_scatter(totals, ('dp', 'ctx'), scatter_dimension=0, tiled=True)  283 us
    convert_element_type x2, other arithmetic, on_device(): d_scores = (probs * (d_probs - row_sums)).astype(jnp.bfloat16)  80.9 us
    unnamed x2, blocking collectives  80.6 us
    dot_general x2, matrix products, on_device(): jnp.einsum('qhd,khd->hqk', d_mixed, value_heads, preferred_element_type=j...  76.5 us
    dot_general x12, matrix products, matmul(): return jnp.dot(left, right, preferred_element_type=jnp.float32)  71.8 us
    all_gather x1, waiting for transfers between devices, fetch_weights(): lax.all_gather(shards[2], ('dp', 'ctx'), axis=0, tiled=True)  58.2 us
    dot_general x2, matrix products, on_device(): jnp.einsum('hqk,qhd->khd', probs_low, d_mixed, preferred_element_type=jnp...  45.5 us
  transfers between devices with their start and end apart: 20, of which 13 were waited for; matrix products, arithmetic and copies ran while one was open for 35% of the time, Pallas kernels for 0%

commit v1 on v0

--- a/solution.py
+++ b/solution.py
@@ -7,6 +7,19 @@
 HEADS = 12
 HEAD = 64
 epsilon = 1e-05
+
+
+def collect(array, axis, dim):
+    ways = lax.axis_size(axis)
+    up = [(d, (d + 1) % ways) for d in range(ways)]
+    down = [(d, (d - 1) % ways) for d in range(ways)]
+    earlier, later = ([array], [array])
+    for _ in range(ways // 2):
+        earlier.append(lax.ppermute(earlier[-1], axis, up))
+    for _ in range((ways - 1) // 2):
+        later.append(lax.ppermute(later[-1], axis, down))
+    line = jnp.concatenate([*earlier[::-1], *later[1:]], axis=dim)
+    return jnp.roll(line, (lax.axis_index(axis) - ways // 2) * array.shape[dim], axis=dim)
 
 
 def layer_norm(values, gain, shift):
@@ -113,7 +126,7 @@
             jnp.bfloat16
         )
         keys_whole, values_whole = (
-            lax.all_gather(keys_local, "ctx", axis=0, tiled=True),
+            collect(keys_local, "ctx", 0),
             lax.all_gather(values_local, "ctx", axis=0, tiled=True),
         )
         query_heads = queries.reshape(local, HEADS, HEAD)

time: 1540 us -> 1490 us (0.968)
  waiting for transfers between devices: 801 us -> 717 us
  other arithmetic: 145 us -> 168 us
    all_gather x2 -> x0, waiting for transfers between devices: 43.7 us -> none  [on_device(): lax.all_gather(keys_local, 'ctx', axis=0, tiled=True)]
    ppermute x0 -> x6, waiting for transfers between devices: none -> 22.6 us  [the longest x4 22.6 us: collect(): earlier.append(lax.ppermute(earlier[-1], axis, up))]
    concatenate x0 -> x2, other arithmetic: none -> 21.8 us  [collect(): jnp.roll(line, (lax.axis_index(axis) - ways // 2) * array.shape[dim], axi...]
    all_gather x1, waiting for transfers between devices: 19.2 us -> 0.02 us  [fetch_weights(): lax.all_gather(shards[9], ('dp', 'ctx'), axis=0, tiled=True)]
    unnamed x234 -> x218, local copies, waits for them, and re-layouts: 29.8 us -> 35.3 us
    unnamed x23 -> x21, waiting for transfers between devices: 309 us -> 310 us
  transfers between devices with their start and end apart: 20 -> 24, of which waited for: 13 -> 11; matrix products, arithmetic and copies ran while one was open for 35% -> 38% of each run, Pallas kernels for 0% -> 0%
where the time goes in v1:
time: 1490 us; the launch traced here: 1480 us
  waiting for transfers between devices  717 us (48%)
  matrix products  434 us (29%)
  other arithmetic  168 us (11%)
  blocking collectives  82.8 us (6%)
  local copies, waits for them, and re-layouts  59.8 us (4%)
  between operations  16.1 us (1%)
    unnamed x21, waiting for transfers between devices  310 us
    reduce_scatter x3, waiting for transfers between devices, on_device(): lax.psum_scatter(totals, ('dp', 'ctx'), scatter_dimension=0, tiled=True)  283 us
    unnamed x2, blocking collectives  82.8 us
    convert_element_type x2, other arithmetic, on_device(): d_scores = (probs * (d_probs - row_sums)).astype(jnp.bfloat16)  81 us
    dot_general x2, matrix products, on_device(): jnp.einsum('qhd,khd->hqk', d_mixed, value_heads, preferred_element_type=j...  76.6 us
    dot_general x12, matrix products, matmul(): return jnp.dot(left, right, preferred_element_type=jnp.float32)  71.9 us
    all_gather x1, waiting for transfers between devices, fetch_weights(): lax.all_gather(shards[2], ('dp', 'ctx'), axis=0, tiled=True)  48.4 us
    dot_general x2, matrix products, on_device(): jnp.einsum('hqk,qhd->khd', probs_low, d_mixed, preferred_element_type=jnp...  45.6 us
  transfers between devices with their start and end apart: 24, of which 11 were waited for; matrix products, arithmetic and copies ran while one was open for 38% of the time, Pallas kernels for 0%

profile of v1, /device:TPU:0, one launch (start us, length us, event | category | flops | bytes accessed | tf_op | source)
XLA Modules:
  0.0 1482.0 jit_solution(12422888459164691713)
XLA Ops:
  17.0 42.5 %all-reduce.19 = (bf16[768]{0:T(1024)(128)(2,1)S(1)}, bf16[768]{0:T(1024)(128)(2,1)S(1)}, bf16[768]{0:T(1024)(128)(2,1)S(1)}, bf16[768]{0:T(1024)(128)(2,1)S(1)}...) all-reduce(bf16[768]{0:T(1024)(128)(2,1)S(1)} %dynamic-update-slice, ...), channel_id=1, replica_groups=mesh['dp'=8,'ctx'=4] {'dp','ctx'}, use_global_device_ids=true, to_apply=%add | all-reduce | flops 9216 | bytes 36864
  59.5 8.4 all-gather.9.cloned.1.call-done
  75.3 48.4 %all-gather.15.cloned.1.call-done = bf16[768,768]{1,0:T(8,128)(2,1)} async-done(((bf16[24,768]{1,0:T(8,128)(2,1)}), bf16[768,768]{1,0:T(8,128)(2,1)}) %all-gather.15.cloned.1.call-update) | async-done | bytes 1179664 | tf_op jit(solution)/shard_map/all_gather | solution.py:40
  132.1 12.6 collective-permute-done
  149.1 31.9 %all-gather.13.cloned.1.call-done = bf16[768,768]{1,0:T(8,128)(2,1)} async-done(((bf16[24,768]{1,0:T(8,128)(2,1)}), bf16[768,768]{1,0:T(8,128)(2,1)}) %all-gather.13.cloned.1.call-update) | async-done | bytes 1179664 | tf_op jit(solution)/shard_map/all_gather | solution.py:38
  191.8 10.9 fusion.26
  202.7 4.7 copy.63
  207.4 10.0 collective-permute-done.4
  217.4 10.9 fusion.19
  228.3 4.7 copy.66
  233.0 22.7 %fusion.1 = (f32[12,512]{1,0:T(8,128)S(1)}, f32[12,512,2048]{2,1,0:T(8,128)}) fusion(pred[512,2048]{1,0:T(8,128)(4,1)S(1)} %broadcast_compare_fusion, bf16[512,12,64]{0,2,1:T(8,128)(2,1)S(1)} %bitcast.203, bf16[2048,12,64]{0,2,1:T(8,128)(2,1)} %bitcast.195), kind=kOutput, calls=%fused_computation.11 | convolution fusion | flops 1648355328 | bytes 55336960 | tf_op jit(solution)/shard_map/qhd,khd->hqk/dot_general | solution.py:58
  255.8 22.1 %exponential_reduce_fusion = f32[12,512]{1,0:T(8,128)S(1)} fusion(f32[12,512,2048]{2,1,0:T(8,128)} %get-tuple-element.146, f32[12,512]{1,0:T(8,128)S(1)} %get-tuple-element.145, pred[512,2048]{1,0:T(8,128)(4,1)S(1)} %broadcast_compare_fusion), kind=kLoop, calls=%fused_computation.5 | loop fusion | flops 50325504 | bytes 51429376 | tf_op jit(solution)/shard_map/reduce_sum | solution.py:137
  277.9 22.5 %fusion = (f32[12,512]{1,0:T(8,128)S(1)}, f32[12,512,2048]{2,1,0:T(8,128)}) fusion(pred[512,2048]{1,0:T(8,128)(4,1)S(1)} %broadcast_compare_fusion.1, bf16[512,12,64]{0,2,1:T(8,128)(2,1)S(1)} %bitcast.205, bf16[2048,12,64]{0,2,1:T(8,128)(2,1)} %bitcast.193), kind=kOutput, calls=%fused_computation.10 | convolution fusion | flops 1648355328 | bytes 55336960 | tf_op jit(solution)/shard_map/qhd,khd->hqk/dot_general | solution.py:58
  300.4 22.0 %exponential_reduce_fusion.1 = f32[12,512]{1,0:T(8,128)S(1)} fusion(f32[12,512,2048]{2,1,0:T(8,128)} %get-tuple-element.142, f32[12,512]{1,0:T(8,128)S(1)} %get-tuple-element.141, pred[512,2048]{1,0:T(8,128)(4,1)S(1)} %broadcast_compare_fusion.1), kind=kLoop, calls=%fused_computation.8 | loop fusion | flops 50325504 | bytes 51429376 | tf_op jit(solution)/shard_map/reduce_sum | solution.py:137
  322.4 4.6 copy.64
  327.1 20.6 %convolution_convert_fusion.2 = bf16[12,64,512]{2,1,0:T(8,128)(2,1)S(1)} fusion(bf16[2048,12,64]{0,2,1:T(8,128)(2,1)} %bitcast.197, f32[12,512,2048]{2,1,0:T(8,128)} %get-tuple-element.146, f32[12,512]{1,0:T(8,128)S(1)} %log_add_fusion, pred[512,2048]{1,0:T(8,128)(4,1)S(1)} %broadcast_compare_fusion), kind=kOutput, calls=%fused_computation.152 | convolution fusion | flops 1661337600 | bytes 55336960 | tf_op jit(solution)/shard_map/hqk,khd->qhd/dot_general | solution.py:140
  351.4 4.7 copy.61
  356.1 21.0 %convolution_convert_fusion.3 = bf16[12,64,512]{2,1,0:T(8,128)(2,1)S(1)} fusion(bf16[2048,12,64]{0,2,1:T(8,128)(2,1)} %bitcast.199, f32[12,512,2048]{2,1,0:T(8,128)} %get-tuple-element.142, f32[12,512]{1,0:T(8,128)S(1)} %log_add_fusion.1, pred[512,2048]{1,0:T(8,128)(4,1)S(1)} %broadcast_compare_fusion.1), kind=kOutput, calls=%fused_computation.153 | convolution fusion | flops 1661337600 | bytes 55336960 | tf_op jit(solution)/shard_map/hqk,khd->qhd/dot_general | solution.py:140
  379.7 5.4 fusion.90
  387.8 34.9 %multiply_convert_fusion.5 = (bf16[512,3072]{1,0:T(8,128)(2,1)}, f32[512,3072]{1,0:T(8,128)}, bf16[512,3072]{1,0:T(8,128)(2,1)}, f32[512,3072]{1,0:T(8,128)}, f32[512,3072]{1,0:T(8,128)}) fusion(f32[3072]{0:T(1024)S(1)} %convert_element_type.260, f32[512,3072]{1,0:T(8,128)S(1)} %fusion.90, bf16[768,3072]{1,0:T(8,128)(2,1)S(1)} %copy-done.85, ...), kind=kOutput, calls=%fused_computation.53 | convolution fusion | flops 2625503232 | bytes 37771264 | tf_op jit(solution)/shard_map/dot_general | solution.py:65
  422.7 12.7 all-gather.21.cloned.1.call-done
  435.4 6.6 fusion.105
  452.8 5.0 fusion.109
  457.8 17.7 %convert_reduce_fusion.1 = (f32[3072]{0:T(1024)}, bf16[512,3072]{1,0:T(8,128)(2,1)}, f32[3072]{0:T(1024)}, bf16[512,3072]{1,0:T(8,128)(2,1)}) fusion(f32[512,3072]{1,0:T(8,128)} %get-tuple-element.122, f32[512,3072]{1,0:T(8,128)} %get-tuple-element.149, f32[3072]{0:T(1024)S(1)} %convert_element_type.260, f32[512,3072]{1,0:T(8,128)} %fusion.109, ...), kind=kOutput, calls=%fused_computation.35 | convolution fusion | flops 2469390336 | bytes 43290624 | tf_op jit(solution)/shard_map/td,fd->tf/dot_general | solution.py:182
  475.5 6.5 add_add_fusion.8
  482.0 6.4 multiply_reduce_fusion.3
  494.7 22.6 %convolution_convert_fusion.1 = bf16[12,64,2048]{2,1,0:T(8,128)(2,1)} fusion(bf16[512,12,64]{0,2,1:T(8,128)(2,1)S(1)} %bitcast.213, f32[12,512,2048]{2,1,0:T(8,128)} %get-tuple-element.142, f32[12,512]{1,0:T(8,128)S(1)} %log_add_fusion.1, pred[512,2048]{1,0:T(8,128)(4,1)S(1)} %broadcast_compare_fusion.1), kind=kOutput, calls=%fused_computation.71 | convolution fusion | flops 1662517248 | bytes 55336960 | tf_op jit(solution)/shard_map/hqk,qhd->khd/dot_general | solution.py:222
  525.3 22.9 %convolution_convert_fusion = bf16[12,64,2048]{2,1,0:T(8,128)(2,1)} fusion(bf16[512,12,64]{0,2,1:T(8,128)(2,1)S(1)} %bitcast.211, f32[12,512,2048]{2,1,0:T(8,128)} %get-tuple-element.146, f32[12,512]{1,0:T(8,128)S(1)} %copy-done.52, pred[512,2048]{1,0:T(8,128)(4,1)S(1)} %copy-done.1), kind=kOutput, calls=%fused_computation.70 | convolution fusion | flops 1662517248 | bytes 55336960 | tf_op jit(solution)/shard_map/hqk,qhd->khd/dot_general | solution.py:222
  549.4 37.9 %multiply_reduce_fusion.1 = (f32[12,512]{1,0:T(8,128)S(1)}, f32[12,512,2048]{2,1,0:T(8,128)}) fusion(f32[12,512,2048]{2,1,0:T(8,128)} %get-tuple-element.142, f32[12,512]{1,0:T(8,128)S(1)} %log_add_fusion.1, pred[512,2048]{1,0:T(8,128)(4,1)S(1)} %broadcast_compare_fusion.1, bf16[512,12,64]{0,2,1:T(8,128)(2,1)S(1)} %bitcast.214, ...), kind=kOutput, calls=%fused_computation.3 | convolution fusion | flops 1673521152 | bytes 105693184 | tf_op jit(solution)/shard_map/qhd,khd->hqk/dot_general | solution.py:204
  587.3 40.5 %multiply_convert_fusion.1 = bf16[12,512,2048]{2,1,0:T(8,128)(2,1)} fusion(f32[12,512,2048]{2,1,0:T(8,128)} %get-tuple-element.158, f32[12,512,2048]{2,1,0:T(8,128)} %get-tuple-element.142, f32[12,512]{1,0:T(8,128)S(1)} %get-tuple-element.157, f32[12,512]{1,0:T(8,128)S(1)} %log_add_fusion.1, pred[512,2048]{1,0:T(8,128)(4,1)S(1)} %broadcast_compare_fusion.1), kind=kLoop, calls=%fused_computation.2 | loop fusion | flops 75497472 | bytes 126926848 | tf_op jit(solution)/shard_map/convert_element_type | solution.py:208
  627.8 14.3 multiply_convert_fusion.3
  643.2 38.8 %multiply_reduce_fusion = (f32[12,512]{1,0:T(8,128)S(1)}, f32[12,512,2048]{2,1,0:T(8,128)}) fusion(f32[12,512,2048]{2,1,0:T(8,128)} %get-tuple-element.146, f32[12,512]{1,0:T(8,128)S(1)} %copy-done.52, pred[512,2048]{1,0:T(8,128)(4,1)S(1)} %copy-done.1, bf16[512,12,64]{0,2,1:T(8,128)(2,1)S(1)} %bitcast.212, bf16[2048,12,64]{0,2,1:T(8,128)(2,1)} %bitcast.198), kind=kOutput, calls=%fused_computation.1 | convolution fusion | flops 1673521152 | bytes 105693184 | tf_op jit(solution)/shard_map/qhd,khd->hqk/dot_general | solution.py:204
  682.0 40.4 %multiply_convert_fusion = bf16[12,512,2048]{2,1,0:T(8,128)(2,1)} fusion(f32[12,512,2048]{2,1,0:T(8,128)} %get-tuple-element.156, f32[12,512,2048]{2,1,0:T(8,128)} %get-tuple-element.146, f32[12,512]{1,0:T(8,128)S(1)} %get-tuple-element.155, f32[12,512]{1,0:T(8,128)S(1)} %copy-done.52, pred[512,2048]{1,0:T(8,128)(4,1)S(1)} %copy-done.1), kind=kLoop, calls=%fused_computation | loop fusion | flops 75497472 | bytes 126926848 | tf_op jit(solution)/shard_map/convert_element_type | solution.py:208
  722.4 14.3 multiply_convert_fusion.2
  742.7 14.2 convert_reduce_fusion.11
  760.6 13.5 convert_reduce_fusion.10
  774.2 4.3 add_bitcast_fusion.2
  785.1 4.2 add_bitcast_fusion
  803.5 5.0 fusion.92
  808.6 5.8 convolution_add_fusion.1
  814.5 5.0 fusion.113
  819.5 5.3 convolution_add_fusion
  832.7 40.3 %all-reduce.18 = (f32[768]{0:T(1024)S(1)}, f32[768]{0:T(1024)S(1)}, f32[768]{0:T(1024)S(1)}, f32[768]{0:T(1024)S(1)}, f32[768]{0:T(1024)S(1)}, /*index=5*/f32[30...) all-reduce(f32[768]{0:T(1024)S(1)} %add.341, ...), channel_id=7, replica_groups=mesh['dp'=8,'ctx'=4] {'dp','ctx'}, use_global_device_ids=true, to_apply=%region_29.31.clone | all-reduce | flops 9216 | bytes 73728
  886.1 96.9 %reduce-scatter.31.cloned.1.call-done = f32[24,768]{1,0:T(8,128)} async-done(((f32[768,768]{1,0:T(8,128)}), f32[24,768]{1,0:T(8,128)}) %reduce-scatter.31.cloned.1.call-update) | async-done | bytes 73744
  983.0 104.4 %reduce-scatter.35.cloned.1.call-done = f32[24,768]{1,0:T(8,128)} async-done(((f32[768,768]{1,0:T(8,128)}), f32[24,768]{1,0:T(8,128)}) %reduce-scatter.35.cloned.1.call-update) | async-done | bytes 73744
  1087.3 104.4 %reduce-scatter.33.cloned.1.call-done = f32[24,768]{1,0:T(8,128)} async-done(((f32[768,768]{1,0:T(8,128)}), f32[24,768]{1,0:T(8,128)}) %reduce-scatter.33.cloned.1.call-update) | async-done | bytes 73744
  1191.7 141.5 %reduce-scatter.27.cloned.1.call-done = f32[24,3072]{1,0:T(8,128)} async-done(((f32[768,3072]{1,0:T(8,128)}), f32[24,3072]{1,0:T(8,128)}) %reduce-scatter.27.cloned.1.call-update) | async-done | bytes 294928 | tf_op jit(solution)/shard_map/reduce_scatter | solution.py:272
  1333.2 141.5 %reduce-scatter.29.cloned.1.call-done = f32[96,768]{1,0:T(8,128)} async-done(((f32[3072,768]{1,0:T(8,128)}), f32[96,768]{1,0:T(8,128)}) %reduce-scatter.29.cloned.1.call-update) | async-done | bytes 294928 | tf_op jit(solution)/shard_map/reduce_scatter | solution.py:272
  (357 shorter events, 127.4 us)
Async XLA Ops:
  7.2 64.7 %copy-start.7 = (bf16[2,512,768]{2,1,0:T(8,128)(2,1)S(1)}, bf16[2,512,768]{2,1,0:T(8,128)(2,1)}, u32[]{:S(2)}) copy-start(bf16[2,512,768]{2,1,0:T(8,128)(2,1)} %param.20) | copy-start | bytes 4718596
  7.2 60.8 %all-gather.9.cloned.1.call-start = ((), (), s32[]{:S(2)}) async-start(), calls=%async_computation.10 | async-start | bytes 1216512 | tf_op jit(solution)/shard_map/all_gather | solution.py:41
  7.9 115.8 %all-gather.15.cloned.1.call-start = ((), (), s32[]{:S(2)}) async-start(), calls=%async_computation.13 | async-start | bytes 1216512 | tf_op jit(solution)/shard_map/all_gather | solution.py:40
  8.7 172.3 %all-gather.13.cloned.1.call-start = ((), (), s32[]{:S(2)}) async-start(), calls=%async_computation.12 | async-start | bytes 1216512 | tf_op jit(solution)/shard_map/all_gather | solution.py:38
  9.4 313.0 %all-gather.23.cloned.1.call-start = ((), (), s32[]{:S(2)}) async-start(), calls=%async_computation.17 | async-start | bytes 3932160 | tf_op jit(solution)/shard_map/all_gather | solution.py:130
  71.3 276.4 %all-gather.17.cloned.1.call-start = ((), (), s32[]{:S(2)}) async-start(), calls=%async_computation.14 | async-start | bytes 1216512 | tf_op jit(solution)/shard_map/all_gather | solution.py:43
  71.9 279.6 %all-gather.11.cloned.1.call-start = ((), (), s32[]{:S(2)}) async-start(), calls=%async_computation.11 | async-start | bytes 3932160 | tf_op jit(solution)/shard_map/all_gather | solution.py:130
  73.7 306.0 %all-gather.19.cloned.1.call-start = ((), (), s32[]{:S(2)}) async-start(), calls=%async_computation.15 | async-start | bytes 4866048 | tf_op jit(solution)/shard_map/all_gather | solution.py:47
  74.4 361.0 %all-gather.21.cloned.1.call-start = ((), (), s32[]{:S(2)}) async-start(), calls=%async_computation.16 | async-start | bytes 4866048 | tf_op jit(solution)/shard_map/all_gather | solution.py:49
  75.2 706.6 %reduce-scatter.19.cloned.1.call-start = ((), (), s32[]{:S(2)}) async-start(), calls=%async_computation.19 | async-start | bytes 3932160 | tf_op jit(solution)/shard_map/reduce_scatter | solution.py:229
  126.8 17.9 %collective-permute-start = (bf16[512,768]{1,0:T(8,128)(2,1)}, bf16[512,768]{1,0:T(8,128)(2,1)}, u32[]{:S(2)}, u32[]{:S(2)}) collective-permute-start(bf16[512,768]{1,0:T(8,128)(2,1)} %convolution_convert_fusion.7), channel_id=1, source_target_pairs={{0,1},{1,2},{2,3},{3,0},{4,5},{5,6},{6,7},{7,4},{8,9},{9,10},{10,1... | collective-permute-start | bytes 2359304 | tf_op jit(solution)/shard_map/ppermute | solution.py:18
  127.7 64.1 %collective-permute-start.2 = (bf16[512,768]{1,0:T(8,128)(2,1)}, bf16[512,768]{1,0:T(8,128)(2,1)}, u32[]{:S(2)}, u32[]{:S(2)}) collective-permute-start(bf16[512,768]{1,0:T(8,128)(2,1)} %convolution_convert_fusion.7), channel_id=1, source_target_pairs={{0,3},{1,0},{2,1},{3,2},{4,7},{5,4},{6,5},{7,6},{8,11},{9,8},{10,9... | collective-permute-start | bytes 2359304 | tf_op jit(solution)/shard_map/ppermute | solution.py:20
  132.1 59.4 %collective-permute-start.3 = (bf16[512,768]{1,0:T(8,128)(2,1)}, bf16[512,768]{1,0:T(8,128)(2,1)}, u32[]{:S(2)}, u32[]{:S(2)}) collective-permute-start(bf16[512,768]{1,0:T(8,128)(2,1)} %convolution_convert_fusion.6), channel_id=1, source_target_pairs={{0,1},{1,2},{2,3},{3,0},{4,5},{5,6},{6,7},{7,4},{8,9},{9,10},{10,1... | collective-permute-start | bytes 2359304 | tf_op jit(solution)/shard_map/ppermute | solution.py:18
  144.7 47.1 %collective-permute-start.1 = (bf16[512,768]{1,0:T(8,128)(2,1)}, bf16[512,768]{1,0:T(8,128)(2,1)}, u32[]{:S(2)}, u32[]{:S(2)}) collective-permute-start(bf16[512,768]{1,0:T(8,128)(2,1)} %collective-permute-done), channel_id=1, source_target_pairs={{0,1},{1,2},{2,3},{3,0},{4,5},{5,6},{6,7},{7,4},{8,9},{9,10},{10,1... | collective-permute-start | bytes 2359304 | tf_op jit(solution)/shard_map/ppermute | solution.py:18
  145.4 181.6 %copy-start = (pred[512,2048]{1,0:T(8,128)(4,1)}, pred[512,2048]{1,0:T(8,128)(4,1)S(1)}, u32[]{:S(2)}) copy-start(pred[512,2048]{1,0:T(8,128)(4,1)S(1)} %broadcast_compare_fusion) | copy-start | bytes 3145732
  145.5 343.0 %copy-start.53 = (f32[768]{0:T(1024)}, f32[768]{0:T(1024)S(1)}, u32[]{:S(2)}) copy-start(f32[768]{0:T(1024)S(1)} %convert_element_type.257) | copy-start | bytes 9220
  145.5 296.9 %copy-start.55 = (f32[768]{0:T(1024)}, f32[768]{0:T(1024)S(1)}, u32[]{:S(2)}) copy-start(f32[768]{0:T(1024)S(1)} %convert_element_type.258) | copy-start | bytes 9220
  147.4 60.0 %collective-permute-start.5 = (bf16[512,768]{1,0:T(8,128)(2,1)}, bf16[512,768]{1,0:T(8,128)(2,1)}, u32[]{:S(2)}, u32[]{:S(2)}) collective-permute-start(bf16[512,768]{1,0:T(8,128)(2,1)} %convolution_convert_fusion.6), channel_id=1, source_target_pairs={{0,3},{1,0},{2,1},{3,2},{4,7},{5,4},{6,5},{7,6},{8,11},{9,8},{10,9... | collective-permute-start | bytes 2359304 | tf_op jit(solution)/shard_map/ppermute | solution.py:20
  185.6 47.5 %copy-start.15 = (bf16[512,768]{0,1:T(8,128)(2,1)}, bf16[512,768]{0,1:T(8,128)(2,1)S(1)}, u32[]{:S(2)}) copy-start(bf16[512,768]{0,1:T(8,128)(2,1)S(1)} %copy.65) | copy-start | bytes 2359300
  191.4 26.0 %collective-permute-start.4 = (bf16[512,768]{1,0:T(8,128)(2,1)}, bf16[512,768]{1,0:T(8,128)(2,1)}, u32[]{:S(2)}, u32[]{:S(2)}) collective-permute-start(bf16[512,768]{1,0:T(8,128)(2,1)} %collective-permute-done.3), channel_id=1, source_target_pairs={{0,1},{1,2},{2,3},{3,0},{4,5},{5,6},{6,7},{7,4},{8,9},{9,10},{10,1... | collective-permute-start | bytes 2359304 | tf_op jit(solution)/shard_map/ppermute | solution.py:18
  255.8 22.1 %copy-start.17 = (bf16[512,768]{0,1:T(8,128)(2,1)S(1)}, bf16[512,768]{0,1:T(8,128)(2,1)}, u32[]{:S(2)}) copy-start(bf16[512,768]{0,1:T(8,128)(2,1)} %copy.62) | copy-start | bytes 2359300
  277.9 49.2 %copy-start.51 = (f32[12,512]{1,0:T(8,128)}, f32[12,512]{1,0:T(8,128)S(1)}, u32[]{:S(2)}) copy-start(f32[12,512]{1,0:T(8,128)S(1)} %log_add_fusion) | copy-start | bytes 73732
  347.6 8.5 copy-start.46
  351.4 137.1 %copy-start.57 = (f32[512]{0:T(512)}, f32[512]{0:T(512)S(1)}, u32[]{:S(2)}) copy-start(f32[512]{0:T(512)S(1)} %broadcast_multiply_fusion.1) | copy-start | bytes 6148
  356.1 21.1 %copy-start.8 = (bf16[2,512,768]{2,1,0:T(8,128)(2,1)S(1)}, bf16[2,512,768]{2,1,0:T(8,128)(2,1)}, u32[]{:S(2)}) copy-start(bf16[2,512,768]{2,1,0:T(8,128)(2,1)} %param.20) | copy-start | bytes 4718596
  356.1 21.1 %copy-start.90 = (bf16[768,768]{1,0:T(8,128)(2,1)S(1)}, bf16[768,768]{1,0:T(8,128)(2,1)}, u32[]{:S(2)}) copy-start(bf16[768,768]{1,0:T(8,128)(2,1)} %all-gather.17.cloned.1.call-done) | copy-start | bytes 3538948
  378.2 110.3 %copy-start.62 = (f32[512]{0:T(512)}, f32[512]{0:T(512)S(1)}, u32[]{:S(2)}) copy-start(f32[512]{0:T(512)S(1)} %broadcast_multiply_fusion.3) | copy-start | bytes 6148
  379.7 108.9 %copy-start.60 = (f32[512]{0:T(512)}, f32[512]{0:T(512)S(1)}, u32[]{:S(2)}) copy-start(f32[512]{0:T(512)S(1)} %fusion.79) | copy-start | bytes 6148
  379.7 108.9 %copy-start.78 = (f32[512]{0:T(512)}, f32[512]{0:T(512)S(1)}, u32[]{:S(2)}) copy-start(f32[512]{0:T(512)S(1)} %fusion.77) | copy-start | bytes 6148
  379.7 8.1 copy-start.24
  379.7 8.1 copy-start.85
  387.8 47.6 %copy-start.84 = (f32[768]{0:T(1024)S(1)}, f32[768]{0:T(1024)}, u32[]{:S(2)}) copy-start(f32[768]{0:T(1024)} %convert_element_type.262) | copy-start | bytes 9220
  435.4 7.0 copy-start.86
  494.7 22.6 %copy-start.36 = (bf16[512,768]{0,1:T(8,128)(2,1)}, bf16[512,768]{0,1:T(8,128)(2,1)S(1)}, u32[]{:S(2)}) copy-start(bf16[512,768]{0,1:T(8,128)(2,1)S(1)} %copy.67) | copy-start | bytes 2359300
  517.3 267.8 %reduce-scatter.23.cloned.1.call-start = ((), (), s32[]{:S(2)}) async-start(), calls=%async_computation.21 | async-start | bytes 3932160 | tf_op jit(solution)/shard_map/reduce_scatter | solution.py:229
  525.3 23.0 %copy-start.34 = (bf16[512,768]{0,1:T(8,128)(2,1)}, bf16[512,768]{0,1:T(8,128)(2,1)S(1)}, u32[]{:S(2)}) copy-start(bf16[512,768]{0,1:T(8,128)(2,1)S(1)} %copy.68) | copy-start | bytes 2359300
  548.3 244.2 %reduce-scatter.17.cloned.1.call-start = ((), (), s32[]{:S(2)}) async-start(), calls=%async_computation.18 | async-start | bytes 3932160 | tf_op jit(solution)/shard_map/reduce_scatter | solution.py:226
  587.3 40.5 %copy-start.18 = (bf16[512,768]{0,1:T(8,128)(2,1)S(1)}, bf16[512,768]{0,1:T(8,128)(2,1)}, u32[]{:S(2)}) copy-start(bf16[512,768]{0,1:T(8,128)(2,1)} %copy.62) | copy-start | bytes 2359300
  642.1 153.7 %reduce-scatter.21.cloned.1.call-start = ((), (), s32[]{:S(2)}) async-start(), calls=%async_computation.20 | async-start | bytes 3932160 | tf_op jit(solution)/shard_map/reduce_scatter | solution.py:226
  682.0 40.4 %copy-start.16 = (bf16[512,768]{0,1:T(8,128)(2,1)S(1)}, bf16[512,768]{0,1:T(8,128)(2,1)}, u32[]{:S(2)}) copy-start(bf16[512,768]{0,1:T(8,128)(2,1)} %copy-done.15) | copy-start | bytes 2359300
  736.7 149.3 %reduce-scatter.25.cloned.1.call-start = ((), (), s32[]{:S(2)}) async-start(), calls=%async_computation.22 | async-start | bytes 2433024 | tf_op jit(solution)/shard_map/reduce_scatter | solution.py:272
  742.7 240.3 %reduce-scatter.31.cloned.1.call-start = ((), (), s32[]{:S(2)}) async-start(), calls=%async_computation.25 | async-start | bytes 2433024
  781.7 305.6 %reduce-scatter.35.cloned.1.call-start = ((), (), s32[]{:S(2)}) async-start(), calls=%async_computation.27 | async-start | bytes 2433024
  792.4 399.3 %reduce-scatter.33.cloned.1.call-start = ((), (), s32[]{:S(2)}) async-start(), calls=%async_computation.26 | async-start | bytes 2433024
  803.2 530.0 %reduce-scatter.27.cloned.1.call-start = ((), (), s32[]{:S(2)}) async-start(), calls=%async_computation.23 | async-start | bytes 9732096 | tf_op jit(solution)/shard_map/reduce_scatter | solution.py:272
  814.4 660.2 %reduce-scatter.29.cloned.1.call-start = ((), (), s32[]{:S(2)}) async-start(), calls=%async_computation.24 | async-start | bytes 9732096 | tf_op jit(solution)/shard_map/reduce_scatter | solution.py:272
  873.0 7.8 copy-start.48
  873.0 7.8 copy-start.88
  (70 other events, 222.0 us)
Sparse Core Ops, SparseCore 0:
  10.9 57.0 all-gather.8
  70.9 52.7 all-gather.14
  126.6 54.3 all-gather.12
  183.0 34.5 all-gather.22
  220.3 54.8 all-gather.16
  276.7 27.4 all-gather.10
  307.1 63.4 all-gather.18
  373.5 61.9 all-gather.20
  517.4 36.0 reduce-scatter.18
  555.9 37.7 reduce-scatter.22
  642.2 36.9 reduce-scatter.16
  736.9 36.0 reduce-scatter.20
  778.8 99.6 reduce-scatter.24
  884.3 98.6 reduce-scatter.30
  988.7 98.6 reduce-scatter.34
  1093.0 98.6 reduce-scatter.32
  1198.0 135.1 reduce-scatter.26
  1339.5 135.0 reduce-scatter.28
